TPU v7x, 256 devices: a whole 4x4x8 slice. The times are simulated.
256 devices in a mesh: site: 8 (over y, core), sector: 32 (over z, x).
Axes of the slice: x: 4, y: 4, z: 8, core: 2. Of those that a mesh axis runs over, the one named last changes fastest.
Arguments:
- env_in: bfloat16 [256, 20, 1024], P('sector'), as said below
- mpo_terms: bfloat16 [4, 20, 20], replicated, may hold values from -1.25 to 1.25
- site_tensors: bfloat16 [8, 256, 4, 1024], P('site', 'sector'), may hold values from -0.75 to 0.75
- route_owner: int32 [8, 256, 4, 1], P('site'), may hold values from 0 to 31; in each aligned block of 32 rows (0 to 31, 32 to 63, ..., all dimensions but the last counted through in order) at most 2 rows name the same one
- route_sector: int32 [8, 256, 4], P('site'), may hold values from 0 to 7
- live_block_extent: int32 [256], P('sector'), may hold values from 8 to 32, as said below
- psi: bfloat16 [8, 256, 1024], P('site', 'sector'), may hold values from -6 to 6
- right_env: bfloat16 [8, 256, 20, 1024], P('site', 'sector'), as said below
Outputs:
- ground: float32 [8, 256, 1024], P('site', 'sector')
- site_energy: float32 [8], P('site')
Inputs may be any that keep to these rules, and one draw needn't show every extreme that they name: `route_owner`: among the rows of one device at one site (8 sectors times 4 states) no owner is named more than 2 times, and some device's rows name one owner exactly 2 times. `live_block_extent`: some sector block is full in every draw. `env_in`: each block is symmetric in its two block indices for every bond index. `right_env`: each block is symmetric in its two block indices for every bond index.
All inputs are finite; a program needn't handle non-finite values.
Results may differ from a plain program's by a relative error of at most 0.03.
Values may be sent and summed in bfloat16 or wider, within the bound.
No kernel may reach another device: no remote copies, remote signals or barrier semaphores. Data moves between devices by JAX's collectives and lax.ppermute only.
A program may use at most 64 MiB of HBM per device.

v0:
```python
import jax
import jax.numpy as jnp
from jax import lax
from jax.sharding import PartitionSpec as P

B = 32
W_BOND = 20
PHYS = 4
DAV_ITERS = 2


epsilon = 1e-06


def from_behind(block, axis, distance):
    devices = range(lax.axis_size(axis))
    route = [(i - distance, i) for i in devices if i - distance in devices]
    return lax.ppermute(block, axis, route)


def spread(values):
    return values[:, None, None, None]


def contract(left_env, mpo_terms, tensors):
    sec_count = left_env.shape[0]
    env_blocks = left_env.reshape(sec_count, W_BOND, B, B)
    tensor_blocks = tensors.reshape(sec_count, PHYS, B, B)
    mixed = jnp.einsum(
        "swab,pwv->spvab", env_blocks, mpo_terms, preferred_element_type=jnp.float32
    ).astype(jnp.bfloat16)
    halfway = jnp.einsum(
        "spvab,spbc->spvac", mixed, tensor_blocks, preferred_element_type=jnp.float32
    ).astype(jnp.bfloat16)
    return jnp.einsum(
        "spad,spvac->spvdc", tensor_blocks, halfway, preferred_element_type=jnp.float32
    ).astype(jnp.bfloat16)


def slot_ranks(owner_grid):
    site_positions = jnp.arange(owner_grid.shape[1])
    earlier = site_positions[None, :] < site_positions[:, None]
    same_owner = owner_grid[:, :, None] == owner_grid[:, None, :]
    return jnp.sum(jnp.where(same_owner & earlier[None], 1, 0), axis=2).astype(jnp.int32)


def local_sum(former, latter):
    return jnp.sum(former * latter, axis=(1, 2, 3))


def rayleigh(trial_vector, image, count_all):
    return lax.psum(local_sum(trial_vector, image), "sector") / count_all


def local(
    env_in, mpo_terms, site_tensors, route_owner, route_sector, live_block_extent, psi, right_env
):
    n_sector = lax.axis_size("sector")
    n_site = lax.axis_size("site")
    member = lax.axis_index("sector")
    segment_index = lax.axis_index("site")
    sites_dev = site_tensors.shape[0]
    sec_dev = site_tensors.shape[1]
    state_count = site_tensors.shape[2]
    sector_total = sec_dev * n_sector
    row_count = sec_dev * state_count
    capacity = max(2, 2 * row_count // n_sector)
    owners = route_owner[..., 0]
    env_shape = (sec_dev, W_BOND, B * B)

    def route(blocks, site_local):
        flat_blocks = blocks.reshape(row_count, W_BOND * B * B)
        owner_grid = owners[site_local].reshape(n_sector, row_count)
        worker_grid = route_sector[site_local].reshape(n_sector, row_count)
        rank_grid = slot_ranks(owner_grid)
        own_row = lax.dynamic_index_in_dim(owner_grid, member, 0, keepdims=False)
        rank_row = lax.dynamic_index_in_dim(rank_grid, member, 0, keepdims=False)
        send_pick = (
            (own_row[None, None, :] == jnp.arange(n_sector)[:, None, None])
            & (rank_row[None, None, :] == jnp.arange(capacity)[None, :, None])
        ).astype(jnp.bfloat16)
        outbox = jnp.einsum(
            "ocr,rk->ock", send_pick, flat_blocks, preferred_element_type=jnp.float32
        ).astype(jnp.bfloat16)
        inbox = lax.all_to_all(outbox, "sector", split_axis=0, concat_axis=0, tiled=True)
        taken = (owner_grid == member)[None] & (
            worker_grid[None] == jnp.arange(sec_dev)[:, None, None]
        )
        slot_match = rank_grid[None, :, None, :] == jnp.arange(capacity)[None, None, :, None]
        receive_pick = jnp.sum(
            jnp.where(taken[:, :, None, :] & slot_match, 1.0, 0.0), axis=3
        ).astype(jnp.bfloat16)
        summed = jnp.einsum(
            "tpc,pck->tk", receive_pick, inbox, preferred_element_type=jnp.float32
        ).astype(jnp.bfloat16)
        return summed.reshape(env_shape)

    def segment(left_env):
        entering = [left_env]
        left_env = route(contract(left_env, mpo_terms, site_tensors[0]), 0)
        return (left_env, jnp.stack(entering))

    first_env = jnp.where(segment_index == 0, env_in, jnp.zeros_like(env_in))

    def advance(turn, current):
        leaving, unused = segment(current)
        moved = from_behind(leaving, "site", 1)
        return jnp.where(segment_index == 0, env_in, moved)

    current_env = lax.fori_loop(0, n_site - 1, advance, first_env)
    unused_env, left_environments = segment(current_env)
    site_positions = jnp.arange(B, dtype=jnp.int32)
    live_flags = site_positions[None, :] < live_block_extent[:, None]
    sector_block_mask = (live_flags[:, :, None] & live_flags[:, None, :]).astype(jnp.float32)
    left_full = left_environments.astype(jnp.float32).reshape(sites_dev, sec_dev, W_BOND, B, B)
    right_full = right_env.astype(jnp.float32).reshape(sites_dev, sec_dev, W_BOND, B, B)
    count_all = float(sector_total * B * B)

    def operate(field):
        product = jnp.einsum("nswab,nsbc->nswac", left_full, field, precision=lax.Precision.HIGHEST)
        product = jnp.einsum(
            "nswac,nswcd->nsad", product, right_full, precision=lax.Precision.HIGHEST
        )
        return product * sector_block_mask

    left_diag = jnp.diagonal(left_full, axis1=3, axis2=4)
    right_diag = jnp.diagonal(right_full, axis1=3, axis2=4)
    precond = jnp.einsum("nswa,nswb->nsab", left_diag, right_diag, precision=lax.Precision.HIGHEST)
    start = psi.astype(jnp.float32).reshape(sites_dev, sec_dev, B, B) * sector_block_mask
    start_norm = lax.psum(local_sum(start, start), "sector") / count_all
    trial_vector = start / spread(jnp.sqrt(start_norm + epsilon))
    image = operate(trial_vector)
    energy = rayleigh(trial_vector, image, count_all)
    for sweep_index in range(DAV_ITERS):
        residual_vector = image - spread(energy) * trial_vector
        correction = residual_vector / jnp.maximum(precond - spread(energy), 1.0)
        correlation = lax.psum(local_sum(trial_vector, correction), "sector") / count_all
        orthogonal = correction - spread(correlation) * trial_vector
        length_sq = lax.psum(local_sum(orthogonal, orthogonal), "sector") / count_all
        direction = orthogonal / spread(jnp.sqrt(length_sq + epsilon))
        applied = operate(direction)
        coupling_sum, curvature_sum = lax.psum(
            (local_sum(direction, image), local_sum(direction, applied)), "sector"
        )
        coupling = coupling_sum / count_all
        curvature = curvature_sum / count_all
        angle = 0.5 * jnp.arctan2(-2.0 * coupling, curvature - energy)
        trial_vector = spread(jnp.cos(angle)) * trial_vector + spread(jnp.sin(angle)) * direction
        image = spread(jnp.cos(angle)) * image + spread(jnp.sin(angle)) * applied
        energy = rayleigh(trial_vector, image, count_all)
    return (trial_vector.reshape(sites_dev, sec_dev, B * B), energy)


def solution(mesh):
    in_specs = (
        P("sector", None, None),
        P(),
        P("site", "sector", None, None),
        P("site", None, None, None),
        P("site", None, None),
        P("sector"),
        P("site", "sector", None),
        P("site", "sector", None, None),
    )
    out_specs = (P("site", "sector", None), P("site"))
    return jax.shard_map(local, mesh=mesh, in_specs=in_specs, out_specs=out_specs, check_vma=False)
```

profile of v0, /device:TPU:16, one launch (start us, length us, event | category | flops | bytes accessed | tf_op | source)
XLA Modules:
  0.0 1507.7 jit_solution(12059380067293907990)
XLA Ops:
  4.5 744.0 %while.18 = (s32[]{:T(128)}, bf16[8,20,1024]{2,0,1:T(8,128)(2,1)S(1)}, pred[]{:T(512)}, s32[1,32]{1,0:T(1,128)S(1)}, s32[1,32]{1,0:T(1,128)S(1)}, /*index=5*/bf1...) while((s32[]{:T(128)}, ...), condition=%wide.region_3.4_spmd, body=%wide.region_2.3_spmd.sunk | while | flops 218565696 | bytes 31333032 | solution.py:110
  17.5 7.9 copy.102
  25.4 7.0 reshape.397
  36.0 73.9 %all_to_all.14 = bf16[32,2,20480]{2,1,0:T(2,128)(2,1)S(1)} all-to-all(bf16[32,2,20480]{2,1,0:T(2,128)(2,1)S(1)} %copy.103), channel_id=1, replica_groups=mesh['site'=8,'sector'=32] {'sector'}, dimensions={0} | all-to-all | bytes 5242880 | tf_op jit(solution)/shard_map/while/body/eval_jaxpr/all_to_all | solution.py:85
  132.9 7.9 copy.102
  140.9 7.0 reshape.397
  151.4 66.1 %all_to_all.14 = bf16[32,2,20480]{2,1,0:T(2,128)(2,1)S(1)} all-to-all(bf16[32,2,20480]{2,1,0:T(2,128)(2,1)S(1)} %copy.103), channel_id=1, replica_groups=mesh['site'=8,'sector'=32] {'sector'}, dimensions={0} | all-to-all | bytes 5242880 | tf_op jit(solution)/shard_map/while/body/eval_jaxpr/all_to_all | solution.py:85
  240.5 7.9 copy.102
  248.4 7.0 reshape.397
  259.0 63.9 %all_to_all.14 = bf16[32,2,20480]{2,1,0:T(2,128)(2,1)S(1)} all-to-all(bf16[32,2,20480]{2,1,0:T(2,128)(2,1)S(1)} %copy.103), channel_id=1, replica_groups=mesh['site'=8,'sector'=32] {'sector'}, dimensions={0} | all-to-all | bytes 5242880 | tf_op jit(solution)/shard_map/while/body/eval_jaxpr/all_to_all | solution.py:85
  345.8 7.9 copy.102
  353.8 7.0 reshape.397
  364.3 62.5 %all_to_all.14 = bf16[32,2,20480]{2,1,0:T(2,128)(2,1)S(1)} all-to-all(bf16[32,2,20480]{2,1,0:T(2,128)(2,1)S(1)} %copy.103), channel_id=1, replica_groups=mesh['site'=8,'sector'=32] {'sector'}, dimensions={0} | all-to-all | bytes 5242880 | tf_op jit(solution)/shard_map/while/body/eval_jaxpr/all_to_all | solution.py:85
  449.8 7.9 copy.102
  457.7 7.0 reshape.397
  468.3 62.4 %all_to_all.14 = bf16[32,2,20480]{2,1,0:T(2,128)(2,1)S(1)} all-to-all(bf16[32,2,20480]{2,1,0:T(2,128)(2,1)S(1)} %copy.103), channel_id=1, replica_groups=mesh['site'=8,'sector'=32] {'sector'}, dimensions={0} | all-to-all | bytes 5242880 | tf_op jit(solution)/shard_map/while/body/eval_jaxpr/all_to_all | solution.py:85
  553.7 7.9 copy.102
  561.6 7.0 reshape.397
  572.2 62.4 %all_to_all.14 = bf16[32,2,20480]{2,1,0:T(2,128)(2,1)S(1)} all-to-all(bf16[32,2,20480]{2,1,0:T(2,128)(2,1)S(1)} %copy.103), channel_id=1, replica_groups=mesh['site'=8,'sector'=32] {'sector'}, dimensions={0} | all-to-all | bytes 5242880 | tf_op jit(solution)/shard_map/while/body/eval_jaxpr/all_to_all | solution.py:85
  657.6 7.9 copy.102
  665.5 7.0 reshape.397
  676.1 62.4 %all_to_all.14 = bf16[32,2,20480]{2,1,0:T(2,128)(2,1)S(1)} all-to-all(bf16[32,2,20480]{2,1,0:T(2,128)(2,1)S(1)} %copy.103), channel_id=1, replica_groups=mesh['site'=8,'sector'=32] {'sector'}, dimensions={0} | all-to-all | bytes 5242880 | tf_op jit(solution)/shard_map/while/body/eval_jaxpr/all_to_all | solution.py:85
  753.8 70.8 %psum.84 = f32[1]{0:T(128)} all-reduce(f32[1]{0:T(128)} %bitcast.12), channel_id=1, replica_groups=mesh['site'=8,'sector'=32] {'sector'}, use_global_device_ids=true, to_apply=%region_5.6 | all-reduce | flops 1 | bytes 8 | tf_op jit(solution)/shard_map/psum | solution.py:130
  840.5 71.7 %psum.85 = f32[1]{0:T(128)} all-reduce(f32[1]{0:T(128)} %bitcast.19), channel_id=1, replica_groups=mesh['site'=8,'sector'=32] {'sector'}, use_global_device_ids=true, to_apply=%region_7.8 | all-reduce | flops 1 | bytes 8 | tf_op jit(solution)/shard_map/psum | solution.py:52
  918.1 70.7 %psum.86 = f32[1]{0:T(128)} all-reduce(f32[1]{0:T(128)} %bitcast.24), channel_id=1, replica_groups=mesh['site'=8,'sector'=32] {'sector'}, use_global_device_ids=true, to_apply=%region_9.10 | all-reduce | flops 1 | bytes 8 | tf_op jit(solution)/shard_map/psum | solution.py:137
  990.2 71.6 %psum.87 = f32[1]{0:T(128)} all-reduce(f32[1]{0:T(128)} %bitcast.26), channel_id=1, replica_groups=mesh['site'=8,'sector'=32] {'sector'}, use_global_device_ids=true, to_apply=%region_11.12 | all-reduce | flops 1 | bytes 8 | tf_op jit(solution)/shard_map/psum | solution.py:139
  1066.5 70.7 %all-reduce.1 = (f32[1]{0:T(128)}, f32[1]{0:T(128)}) all-reduce(f32[1]{0:T(128)} %bitcast.28, f32[1]{0:T(128)} %bitcast.33), channel_id=1, replica_groups=mesh['site'=8,'sector'=32] {'sector'}, use_global_device_ids=true, to_apply=%region_13.14 | all-reduce | flops 2 | bytes 16 | tf_op jit(solution)/shard_map/psum | solution.py:142
  1139.5 71.6 %psum.90 = f32[1]{0:T(128)} all-reduce(f32[1]{0:T(128)} %bitcast.36), channel_id=1, replica_groups=mesh['site'=8,'sector'=32] {'sector'}, use_global_device_ids=true, to_apply=%region_17.18 | all-reduce | flops 1 | bytes 8 | tf_op jit(solution)/shard_map/psum | solution.py:52
  1212.3 70.8 %psum.91 = f32[1]{0:T(128)} all-reduce(f32[1]{0:T(128)} %bitcast.38), channel_id=1, replica_groups=mesh['site'=8,'sector'=32] {'sector'}, use_global_device_ids=true, to_apply=%region_19.20 | all-reduce | flops 1 | bytes 8 | tf_op jit(solution)/shard_map/psum | solution.py:137
  1284.5 71.6 %psum.92 = f32[1]{0:T(128)} all-reduce(f32[1]{0:T(128)} %bitcast.40), channel_id=1, replica_groups=mesh['site'=8,'sector'=32] {'sector'}, use_global_device_ids=true, to_apply=%region_21.22 | all-reduce | flops 1 | bytes 8 | tf_op jit(solution)/shard_map/psum | solution.py:139
  1360.7 70.8 %all-reduce = (f32[1]{0:T(128)}, f32[1]{0:T(128)}) all-reduce(f32[1]{0:T(128)} %bitcast.42, f32[1]{0:T(128)} %bitcast.47), channel_id=1, replica_groups=mesh['site'=8,'sector'=32] {'sector'}, use_global_device_ids=true, to_apply=%region_23.24 | all-reduce | flops 2 | bytes 16 | tf_op jit(solution)/shard_map/psum | solution.py:142
  1434.4 71.5 %psum.95 = f32[1]{0:T(128)} all-reduce(f32[1]{0:T(128)} %bitcast.50), channel_id=1, replica_groups=mesh['site'=8,'sector'=32] {'sector'}, use_global_device_ids=true, to_apply=%region_27.28 | all-reduce | flops 1 | bytes 8 | tf_op jit(solution)/shard_map/psum | solution.py:52
  (145 shorter events, 227.1 us)
Async XLA Ops:
  109.9 9.9 copy-start
  111.4 8.4 collective-permute-start
  217.5 9.9 copy-start
  219.0 8.4 collective-permute-start
  322.9 9.9 copy-start
  324.4 8.4 collective-permute-start
  426.8 9.9 copy-start
  428.3 8.4 collective-permute-start
  530.7 9.9 copy-start
  532.2 8.4 collective-permute-start
  634.6 9.9 copy-start
  636.1 8.4 collective-permute-start
  738.5 9.9 copy-start
  740.0 8.4 collective-permute-start
  748.5 4.4 copy-start.3
  748.5 4.7 copy-start.2
  750.4 78.5 %copy-start.1 = (bf16[8,20,1024]{1,0,2:T(8,128)(2,1)}, bf16[8,20,1024]{1,0,2:T(8,128)(2,1)S(1)}, u32[]{:S(2)}) copy-start(bf16[8,20,1024]{1,0,2:T(8,128)(2,1)S(1)} %copy.53) | copy-start | bytes 983044
where the time goes:
time: 1510 us
  blocking collectives  1170 us (77%)
  local copies, waits for them, and re-layouts  158 us (10%)
  matrix products  109 us (7%)
  waiting for transfers between devices  45.3 us (3%)
    all_to_all x7, blocking collectives, route(): lax.all_to_all(outbox, 'sector', split_axis=0, concat_axis=0, tiled=True)  454 us
    psum x3, blocking collectives, rayleigh(): return lax.psum(local_sum(trial_vector, image), 'sector') / count_all  215 us
    psum x2, blocking collectives, local(): lax.psum(local_sum(orthogonal, orthogonal), 'sector') / count_all  143 us
    psum x2, blocking collectives, local(): lax.psum((local_sum(direction, image), local_sum(direction, applied)), 's...  142 us
    psum x2, blocking collectives, local(): lax.psum(local_sum(trial_vector, correction), 'sector') / count_all  141 us
    psum x1, blocking collectives, local(): start_norm = lax.psum(local_sum(start, start), 'sector') / count_all  70.8 us
    convert_element_type x7, local copies, waits for them, and re-layouts, contract(): return jnp.einsum('spad,spvac->spvdc', tensor_blocks, halfway, preferred_...  55.6 us
    reshape x7, local copies, waits for them, and re-layouts, route(): flat_blocks = blocks.reshape(row_count, W_BOND * B * B)  48.9 us
  transfers between devices with their start and end apart: 7, of which 7 were waited for; matrix products, arithmetic and copies ran while one was open for 0% of the time, Pallas kernels for 0%

commit v1 on v0

--- a/solution.py
+++ b/solution.py
@@ -48,8 +48,13 @@
     return jnp.sum(former * latter, axis=(1, 2, 3))
 
 
-def rayleigh(trial_vector, image, count_all):
-    return lax.psum(local_sum(trial_vector, image), "sector") / count_all
+def sector_sums(parts):
+    n_sector = lax.axis_size("sector")
+    row = jnp.pad(jnp.stack(parts), (0, 128 - len(parts)))
+    sent = jnp.broadcast_to(row[None, None, :], (n_sector, 1, 128))
+    got = lax.all_to_all(sent, "sector", split_axis=0, concat_axis=0, tiled=True)
+    total = jnp.sum(got, axis=(0, 1))
+    return [total[i] for i in range(len(parts))]
 
 
 def local(
@@ -127,27 +132,45 @@
     right_diag = jnp.diagonal(right_full, axis1=3, axis2=4)
     precond = jnp.einsum("nswa,nswb->nsab", left_diag, right_diag, precision=lax.Precision.HIGHEST)
     start = psi.astype(jnp.float32).reshape(sites_dev, sec_dev, B, B) * sector_block_mask
-    start_norm = lax.psum(local_sum(start, start), "sector") / count_all
-    trial_vector = start / spread(jnp.sqrt(start_norm + epsilon))
-    image = operate(trial_vector)
-    energy = rayleigh(trial_vector, image, count_all)
+    def dot(former, latter):
+        return jnp.sum(former * latter)
+
+    raw_image = operate(start)
+    start_norm, raw_energy = sector_sums([dot(start, start), dot(start, raw_image)])
+    start_norm, raw_energy = start_norm / count_all, raw_energy / count_all
+    scale = 1.0 / jnp.sqrt(start_norm + epsilon)
+    trial_vector = start * scale
+    image = raw_image * scale
+    energy = raw_energy * scale * scale
     for sweep_index in range(DAV_ITERS):
-        residual_vector = image - spread(energy) * trial_vector
-        correction = residual_vector / jnp.maximum(precond - spread(energy), 1.0)
-        correlation = lax.psum(local_sum(trial_vector, correction), "sector") / count_all
-        orthogonal = correction - spread(correlation) * trial_vector
-        length_sq = lax.psum(local_sum(orthogonal, orthogonal), "sector") / count_all
-        direction = orthogonal / spread(jnp.sqrt(length_sq + epsilon))
-        applied = operate(direction)
-        coupling_sum, curvature_sum = lax.psum(
-            (local_sum(direction, image), local_sum(direction, applied)), "sector"
+        residual_vector = image - energy * trial_vector
+        correction = residual_vector / jnp.maximum(precond - energy, 1.0)
+        lifted = operate(correction)
+        sums = sector_sums(
+            [
+                dot(trial_vector, correction),
+                dot(correction, correction),
+                dot(trial_vector, trial_vector),
+                dot(correction, image),
+                dot(correction, lifted),
+                dot(trial_vector, lifted),
+                dot(trial_vector, image),
+            ]
         )
-        coupling = coupling_sum / count_all
-        curvature = curvature_sum / count_all
+        vc, cc, vv, ci, cl, vl, vi = [entry / count_all for entry in sums]
+        length_sq = jnp.maximum(cc - 2.0 * vc * vc + vc * vc * vv, 0.0)
+        inverse = 1.0 / jnp.sqrt(length_sq + epsilon)
+        direction = (correction - vc * trial_vector) * inverse
+        applied = (lifted - vc * image) * inverse
+        coupling = (ci - vc * vi) * inverse
+        curvature = (cl - vc * vl - vc * ci + vc * vc * vi) * inverse * inverse
+        crossed = (vl - vc * vi) * inverse
         angle = 0.5 * jnp.arctan2(-2.0 * coupling, curvature - energy)
-        trial_vector = spread(jnp.cos(angle)) * trial_vector + spread(jnp.sin(angle)) * direction
-        image = spread(jnp.cos(angle)) * image + spread(jnp.sin(angle)) * applied
-        energy = rayleigh(trial_vector, image, count_all)
+        cosine, sine = jnp.cos(angle), jnp.sin(angle)
+        trial_vector = cosine * trial_vector + sine * direction
+        image = cosine * image + sine * applied
+        energy = cosine * cosine * vi + cosine * sine * (crossed + coupling) + sine * sine * curvature
+    energy = energy.reshape(1)
     return (trial_vector.reshape(sites_dev, sec_dev, B * B), energy)
 
 

time: 1510 us -> 861 us (0.57)
  blocking collectives: 1170 us -> 481 us
    psum x10 -> x0, blocking collectives: 712 us -> none  [the longest x3 215 us: rayleigh(): return lax.psum(local_sum(trial_vector, image), 'sector') / count_all]
    all_to_all x0 -> x2, blocking collectives: none -> 26.8 us  [sector_sums(): lax.all_to_all(sent, 'sector', split_axis=0, concat_axis=0, tiled=True)]
  transfers between devices with their start and end apart: 7 -> 8, of which waited for: 7 -> 8; matrix products, arithmetic and copies ran while one was open for 0% -> 1% of each run, Pallas kernels for 0% -> 0%
where the time goes in v1:
time: 861 us; the launch traced here: 854 us
  blocking collectives  481 us (56%)
  local copies, waits for them, and re-layouts  170 us (20%)
  matrix products  106 us (12%)
  waiting for transfers between devices  50.4 us (6%)
  between operations  24.2 us (3%)
  starting transfers between devices  17.8 us (2%)
    all_to_all x7, blocking collectives, route(): lax.all_to_all(outbox, 'sector', split_axis=0, concat_axis=0, tiled=True)  454 us
    convert_element_type x7, local copies, waits for them, and re-layouts, contract(): return jnp.einsum('spad,spvac->spvdc', tensor_blocks, halfway, preferred_...  55.6 us
    reshape x7, local copies, waits for them, and re-layouts, route(): flat_blocks = blocks.reshape(row_count, W_BOND * B * B)  48.9 us
    dot_general x7, matrix products, contract(): jnp.einsum('spad,spvac->spvdc', tensor_blocks, halfway, preferred_element...  45.5 us
    ppermute x7, waiting for transfers between devices, from_behind(): return lax.ppermute(block, axis, route)  45.3 us
    dot_general x7, matrix products, contract(): jnp.einsum('swab,pwv->spvab', env_blocks, mpo_terms, preferred_element_ty...  31.5 us
    all_to_all x2, blocking collectives, sector_sums(): lax.all_to_all(sent, 'sector', split_axis=0, concat_axis=0, tiled=True)  26.8 us
    convert_element_type x7, local copies, waits for them, and re-layouts, route(): outbox = jnp.einsum('ocr,rk->ock', send_pick, flat_blocks, preferred_elem...  18.9 us
  transfers between devices with their start and end apart: 8, of which 8 were waited for; matrix products, arithmetic and copies ran while one was open for 1% of the time, Pallas kernels for 0%

profile of v1, /device:TPU:16, one launch (start us, length us, event | category | flops | bytes accessed | tf_op | source)
XLA Modules:
  0.0 854.1 jit_solution(17140565096352988814)
XLA Ops:
  4.4 744.0 %while.18 = (s32[]{:T(128)}, bf16[8,20,1024]{2,0,1:T(8,128)(2,1)S(1)}, pred[]{:T(512)}, s32[1,32]{1,0:T(1,128)S(1)}, s32[1,32]{1,0:T(1,128)S(1)}, /*index=5*/bf1...) while((s32[]{:T(128)}, ...), condition=%wide.region_4.5_spmd, body=%wide.region_3.4_spmd.sunk | while | flops 218565696 | bytes 31333032 | solution.py:115
  11.0 6.5 convert_bitcast_fusion.5
  17.5 7.9 copy.125
  25.5 7.0 reshape.406
  36.0 73.9 %all_to_all.31 = bf16[32,2,20480]{2,1,0:T(2,128)(2,1)S(1)} all-to-all(bf16[32,2,20480]{2,1,0:T(2,128)(2,1)S(1)} %copy.126), channel_id=1, replica_groups=mesh['site'=8,'sector'=32] {'sector'}, dimensions={0} | all-to-all | bytes 5242880 | tf_op jit(solution)/shard_map/while/body/eval_jaxpr/all_to_all | solution.py:90
  126.4 6.5 convert_bitcast_fusion.5
  132.9 7.9 copy.125
  140.8 7.0 reshape.406
  151.4 66.1 %all_to_all.31 = bf16[32,2,20480]{2,1,0:T(2,128)(2,1)S(1)} all-to-all(bf16[32,2,20480]{2,1,0:T(2,128)(2,1)S(1)} %copy.126), channel_id=1, replica_groups=mesh['site'=8,'sector'=32] {'sector'}, dimensions={0} | all-to-all | bytes 5242880 | tf_op jit(solution)/shard_map/while/body/eval_jaxpr/all_to_all | solution.py:90
  234.0 6.5 convert_bitcast_fusion.5
  240.5 7.9 copy.125
  248.4 7.0 reshape.406
  259.0 63.9 %all_to_all.31 = bf16[32,2,20480]{2,1,0:T(2,128)(2,1)S(1)} all-to-all(bf16[32,2,20480]{2,1,0:T(2,128)(2,1)S(1)} %copy.126), channel_id=1, replica_groups=mesh['site'=8,'sector'=32] {'sector'}, dimensions={0} | all-to-all | bytes 5242880 | tf_op jit(solution)/shard_map/while/body/eval_jaxpr/all_to_all | solution.py:90
  339.3 6.5 convert_bitcast_fusion.5
  345.8 7.9 copy.125
  353.8 7.0 reshape.406
  364.3 62.5 %all_to_all.31 = bf16[32,2,20480]{2,1,0:T(2,128)(2,1)S(1)} all-to-all(bf16[32,2,20480]{2,1,0:T(2,128)(2,1)S(1)} %copy.126), channel_id=1, replica_groups=mesh['site'=8,'sector'=32] {'sector'}, dimensions={0} | all-to-all | bytes 5242880 | tf_op jit(solution)/shard_map/while/body/eval_jaxpr/all_to_all | solution.py:90
  443.3 6.5 convert_bitcast_fusion.5
  449.8 7.9 copy.125
  457.7 7.0 reshape.406
  468.3 62.4 %all_to_all.31 = bf16[32,2,20480]{2,1,0:T(2,128)(2,1)S(1)} all-to-all(bf16[32,2,20480]{2,1,0:T(2,128)(2,1)S(1)} %copy.126), channel_id=1, replica_groups=mesh['site'=8,'sector'=32] {'sector'}, dimensions={0} | all-to-all | bytes 5242880 | tf_op jit(solution)/shard_map/while/body/eval_jaxpr/all_to_all | solution.py:90
  534.1 6.5 collective-permute-done
  547.2 6.5 convert_bitcast_fusion.5
  553.7 7.9 copy.125
  561.6 7.0 reshape.406
  572.2 62.4 %all_to_all.31 = bf16[32,2,20480]{2,1,0:T(2,128)(2,1)S(1)} all-to-all(bf16[32,2,20480]{2,1,0:T(2,128)(2,1)S(1)} %copy.126), channel_id=1, replica_groups=mesh['site'=8,'sector'=32] {'sector'}, dimensions={0} | all-to-all | bytes 5242880 | tf_op jit(solution)/shard_map/while/body/eval_jaxpr/all_to_all | solution.py:90
  651.1 6.5 convert_bitcast_fusion.5
  657.6 7.9 copy.125
  665.6 7.0 reshape.406
  676.1 62.4 %all_to_all.31 = bf16[32,2,20480]{2,1,0:T(2,128)(2,1)S(1)} all-to-all(bf16[32,2,20480]{2,1,0:T(2,128)(2,1)S(1)} %copy.126), channel_id=1, replica_groups=mesh['site'=8,'sector'=32] {'sector'}, dimensions={0} | all-to-all | bytes 5242880 | tf_op jit(solution)/shard_map/while/body/eval_jaxpr/all_to_all | solution.py:90
  793.6 14.1 %all_to_all.29 = f32[32,1,128]{2,1,0:T(1,128)S(1)} all-to-all(f32[32,1,128]{2,1,0:T(1,128)S(1)} %broadcast_in_dim.89), channel_id=1, replica_groups=mesh['site'=8,'sector'=32] {'sector'}, dimensions={0} | all-to-all | bytes 32768 | tf_op jit(solution)/shard_map/all_to_all | solution.py:55
  828.4 12.7 %all_to_all.30 = f32[32,1,128]{2,1,0:T(1,128)S(1)} all-to-all(f32[32,1,128]{2,1,0:T(1,128)S(1)} %broadcast_in_dim.90), channel_id=1, replica_groups=mesh['site'=8,'sector'=32] {'sector'}, dimensions={0} | all-to-all | bytes 32768 | tf_op jit(solution)/shard_map/all_to_all | solution.py:55
  (149 shorter events, 192.4 us)
Async XLA Ops:
  109.9 9.9 %copy-start = (bf16[8,20,1024]{2,0,1:T(8,128)(2,1)S(1)}, bf16[8,20,1024]{2,0,1:T(8,128)(2,1)}, u32[]{:S(2)}) copy-start(bf16[8,20,1024]{2,0,1:T(8,128)(2,1)} %get-tuple-element.512) | copy-start | bytes 983044 | tf_op jit(solution)/shard_map/while
  111.4 8.4 collective-permute-start
  217.5 9.9 %copy-start = (bf16[8,20,1024]{2,0,1:T(8,128)(2,1)S(1)}, bf16[8,20,1024]{2,0,1:T(8,128)(2,1)}, u32[]{:S(2)}) copy-start(bf16[8,20,1024]{2,0,1:T(8,128)(2,1)} %get-tuple-element.512) | copy-start | bytes 983044 | tf_op jit(solution)/shard_map/while
  219.0 8.4 collective-permute-start
  322.9 9.9 %copy-start = (bf16[8,20,1024]{2,0,1:T(8,128)(2,1)S(1)}, bf16[8,20,1024]{2,0,1:T(8,128)(2,1)}, u32[]{:S(2)}) copy-start(bf16[8,20,1024]{2,0,1:T(8,128)(2,1)} %get-tuple-element.512) | copy-start | bytes 983044 | tf_op jit(solution)/shard_map/while
  324.4 8.4 collective-permute-start
  426.8 9.9 %copy-start = (bf16[8,20,1024]{2,0,1:T(8,128)(2,1)S(1)}, bf16[8,20,1024]{2,0,1:T(8,128)(2,1)}, u32[]{:S(2)}) copy-start(bf16[8,20,1024]{2,0,1:T(8,128)(2,1)} %get-tuple-element.512) | copy-start | bytes 983044 | tf_op jit(solution)/shard_map/while
  428.3 8.4 collective-permute-start
  530.7 9.9 %copy-start = (bf16[8,20,1024]{2,0,1:T(8,128)(2,1)S(1)}, bf16[8,20,1024]{2,0,1:T(8,128)(2,1)}, u32[]{:S(2)}) copy-start(bf16[8,20,1024]{2,0,1:T(8,128)(2,1)} %get-tuple-element.512) | copy-start | bytes 983044 | tf_op jit(solution)/shard_map/while
  532.2 8.4 collective-permute-start
  634.6 9.9 %copy-start = (bf16[8,20,1024]{2,0,1:T(8,128)(2,1)S(1)}, bf16[8,20,1024]{2,0,1:T(8,128)(2,1)}, u32[]{:S(2)}) copy-start(bf16[8,20,1024]{2,0,1:T(8,128)(2,1)} %get-tuple-element.512) | copy-start | bytes 983044 | tf_op jit(solution)/shard_map/while
  636.1 8.4 collective-permute-start
  738.5 9.9 %copy-start = (bf16[8,20,1024]{2,0,1:T(8,128)(2,1)S(1)}, bf16[8,20,1024]{2,0,1:T(8,128)(2,1)}, u32[]{:S(2)}) copy-start(bf16[8,20,1024]{2,0,1:T(8,128)(2,1)} %get-tuple-element.512) | copy-start | bytes 983044 | tf_op jit(solution)/shard_map/while
  740.0 8.4 collective-permute-start
  748.5 4.4 copy-start.3
  750.4 6.9 copy-start.1
  757.2 4.1 copy-start.2
  767.8 14.0 %all-to-all-start.1 = ((f32[32,1,128]{2,1,0:T(1,128)}), f32[32,1,128]{2,1,0:T(1,128)S(1)}, u32[]{:S(2)}, u32[]{:S(2)}) async-start(f32[32,1,128]{2,1,0:T(1,128)} %broadcast_in_dim.88), calls=%async_computation.1 | async-start | bytes 32768 | tf_op jit(solution)/shard_map/all_to_all | solution.py:55
